TPU v7x, 256 devices: a whole 4x4x8 slice. The times are simulated.
256 devices in a mesh: seq: 32 (over x, z), tp: 8 (over y, core).
Axes of the slice: x: 4, y: 4, z: 8, core: 2. Of those that a mesh axis runs over, the one named last changes fastest.
Arguments:
- tokens: bfloat16 [16384, 5376], P('seq'), may hold values from -6 to 6
- query_weight: bfloat16 [5376, 2048], P(None, 'tp')
- key_weight: bfloat16 [5376, 1024], P(None, 'tp')
- value_weight: bfloat16 [5376, 1024], P(None, 'tp'), may hold values from -0.078125 to 0.078125
- query_norm_gain: float32 [128], replicated, as said below
- key_norm_gain: float32 [128], replicated, as said below
- adapter_down_weight: bfloat16 [32, 5376, 64], P('seq', 'tp'), may hold values from -0.078125 to 0.078125
- adapter_up_weight: bfloat16 [32, 64, 2048], P('seq', None, 'tp'), may hold values from -0.75 to 0.75
- token_adapter_index: int32 [16384, 1], P('seq'), may hold values from 0 to 31; in each aligned block of 512 rows (0 to 511, 512 to 1023, ...) at most 32 rows name the same one
- packed_prompt_length: int32 [16], replicated, may hold values from 1 to 2048, 16384 in all
Outputs:
- attended: bfloat16 [16384, 2048], P('seq', 'tp')
Inputs may be any that keep to these rules, and one draw needn't show every extreme that they name: `token_adapter_index`: in each aligned block of 512 rows (the rows of one index of seq) no adapter is named by more than 32 rows, a bound that some block reaches. `packed_prompt_length`: they sum to 16384; the largest is exactly 2048. `query_norm_gain`: positive gains. `key_norm_gain`: positive gains.
All inputs are finite; a program needn't handle non-finite values.
Results may differ from a plain program's by a relative error of at most 0.02.
Values may be sent and summed in bfloat16 or wider, within the bound.
No kernel may reach another device: no remote copies, remote signals or barrier semaphores. Data moves between devices by JAX's collectives and lax.ppermute only.
A program may use at most 64 MiB of HBM per device.

v0:
```python
import jax
import jax.numpy as jnp
from jax import lax
from jax.sharding import PartitionSpec as P

WINDOW = 1024
query_scale = 0.07715167498104596


def passed_along(block, axis, distance):
    devices = range(lax.axis_size(axis))
    route = [(i - distance, i) for i in devices if i - distance in devices]
    return lax.ppermute(block, axis, route)


def make_dispatch(adapter_of, adapter_total, capacity):
    one_hot = (adapter_of[:, None] == jnp.arange(adapter_total, dtype=jnp.int32)[None, :]).astype(
        jnp.int32
    )
    before = jnp.cumsum(one_hot, axis=0) - one_hot
    slot_index = jnp.sum(before * one_hot, axis=1)
    target = adapter_of * capacity + slot_index
    return (
        jnp.arange(adapter_total * capacity, dtype=jnp.int32)[:, None] == target[None, :]
    ).astype(jnp.bfloat16)


def normalize(field, gain):
    return field / jnp.sqrt(jnp.mean(field * field, axis=-1, keepdims=True) + 1e-06) * gain


def rotate(field, positions):
    half = field.shape[-1] // 2
    freq = jnp.exp(
        -(2.0 * jnp.arange(half, dtype=jnp.float32) / field.shape[-1])
        * jnp.log(jnp.float32(10000.0))
    )
    angle = positions[:, None] * freq[None, :]
    cosine = jnp.cos(angle)[:, None, :]
    sine = jnp.sin(angle)[:, None, :]
    first = field[..., :half]
    second = field[..., half:]
    return jnp.concatenate(
        [first * cosine - second * sine, second * cosine + first * sine], axis=-1
    )


def body(
    tokens,
    query_weight,
    key_weight,
    value_weight,
    query_norm_gain,
    key_norm_gain,
    adapter_down_weight,
    adapter_up_weight,
    token_adapter_index,
    packed_prompt_length,
):
    rows = tokens.shape[0]
    head_dim = query_norm_gain.shape[0]
    kv_local = key_weight.shape[1] // head_dim
    q_local = query_weight.shape[1] // head_dim
    groups = q_local // kv_local
    seq_count = lax.axis_size("seq")
    owned_rows = adapter_down_weight.shape[0]
    adapter_total = owned_rows * seq_count
    capacity = 2 * rows // adapter_total
    feature_slice = adapter_down_weight.shape[1]
    seq_index = lax.axis_index("seq")
    tp_index = lax.axis_index("tp")
    dispatch = make_dispatch(token_adapter_index[:, 0], adapter_total, capacity)
    x_part = lax.dynamic_slice_in_dim(tokens, tp_index * feature_slice, feature_slice, 1)
    packed = jnp.dot(dispatch, x_part, preferred_element_type=jnp.float32).astype(jnp.bfloat16)
    down_all, up_all = (
        lax.all_gather(adapter_down_weight, "seq", axis=0, tiled=True),
        lax.all_gather(adapter_up_weight, "seq", axis=0, tiled=True),
    )
    packed = packed.reshape(adapter_total, capacity, feature_slice)
    partial_low = jnp.einsum("acd,adr->acr", packed, down_all, preferred_element_type=jnp.float32)
    low_rank = lax.psum(partial_low, "tp").astype(jnp.bfloat16)
    delta_slots = jnp.einsum(
        "acr,are->ace", low_rank, up_all, preferred_element_type=jnp.float32
    ).astype(jnp.bfloat16)
    delta_slots = delta_slots.reshape(adapter_total * capacity, q_local * head_dim)
    delta_rows = jnp.einsum("st,se->te", dispatch, delta_slots, preferred_element_type=jnp.float32)
    query = jnp.dot(tokens, query_weight, preferred_element_type=jnp.float32) + delta_rows
    keys = jnp.dot(tokens, key_weight, preferred_element_type=jnp.float32)
    values = jnp.dot(tokens, value_weight, preferred_element_type=jnp.float32).astype(jnp.bfloat16)
    positions = seq_index * rows + jnp.arange(rows, dtype=jnp.int32)
    pos_float = positions.astype(jnp.float32)
    query_rot = rotate(
        normalize(query.reshape(rows, q_local, head_dim), query_norm_gain), pos_float
    ).astype(jnp.bfloat16)
    key_rot = rotate(
        normalize(keys.reshape(rows, kv_local, head_dim), key_norm_gain), pos_float
    ).astype(jnp.bfloat16)
    reach = WINDOW // rows
    earlier = []
    for offset in range(reach, 0, -1):
        earlier.append(passed_along((key_rot, values), "seq", offset))
    all_keys = jnp.concatenate([piece[0] for piece in earlier] + [key_rot], axis=0)
    all_values = jnp.concatenate([piece[1] for piece in earlier] + [values], axis=0)
    all_values = all_values.reshape(WINDOW + rows, kv_local, head_dim)
    key_pos = seq_index * rows - WINDOW + jnp.arange(WINDOW + rows, dtype=jnp.int32)
    starts = jnp.cumsum(packed_prompt_length) - packed_prompt_length
    prompt_start = jnp.max(
        jnp.where(starts[None, :] <= positions[:, None], starts[None, :], 0), axis=1
    )
    lower = jnp.maximum(positions - WINDOW + 1, prompt_start)
    allowed = (key_pos[None, :] >= lower[:, None]) & (key_pos[None, :] <= positions[:, None])
    query_four = query_rot.reshape(rows, kv_local, groups, head_dim)
    scores = (
        jnp.einsum("tkgd,skd->kgts", query_four, all_keys, preferred_element_type=jnp.float32)
        * query_scale
    )
    scores = jnp.where(allowed[None, None], scores, jnp.float32(-1e30))
    peak = jnp.max(scores, axis=-1, keepdims=True)
    weights = jnp.exp(scores - peak)
    probs = (weights / jnp.sum(weights, axis=-1, keepdims=True)).astype(jnp.bfloat16)
    mixed = jnp.einsum("kgts,skd->tkgd", probs, all_values, preferred_element_type=jnp.float32)
    return mixed.astype(jnp.bfloat16).reshape(rows, q_local * head_dim)


def solution(mesh):
    in_specs = (
        P("seq", None),
        P(None, "tp"),
        P(None, "tp"),
        P(None, "tp"),
        P(),
        P(),
        P("seq", "tp", None),
        P("seq", None, "tp"),
        P("seq", None),
        P(),
    )
    out_specs = P("seq", "tp")
    return jax.shard_map(body, mesh=mesh, in_specs=in_specs, out_specs=out_specs, check_vma=False)
```

profile of v0, /device:TPU:8, one launch (start us, length us, event | category | flops | bytes accessed | tf_op | source)
XLA Modules:
  0.0 193.4 jit_solution(9777939212335164480)
XLA Ops:
  7.4 5.1 %multiply_reduce_fusion.1 = (f32[512]{0:T(512)S(1)}, f32[512,128]{0,1:T(8,128)S(1)}) fusion(bf16[512,5376]{1,0:T(8,128)(2,1)} %param.10, bf16[5376,128]{1,0:T(8,128)(2,1)} %param.12), kind=kOutput, calls=%fused_computation.43 | convolution fusion | flops 704773632 | bytes 7145472 | tf_op jit(solution)/shard_map/dot_general | solution.py:88
  14.4 5.8 %collective-permute-start.2 = (bf16[512,1,128]{0,2,1:T(8,128)(2,1)}, bf16[512,1,128]{0,2,1:T(8,128)(2,1)}, u32[]{:S(2)}, u32[]{:S(2)}) collective-permute-start(bf16[512,1,128]{0,2,1:T(8,128)(2,1)} %pad_maximum_fusion), channel_id=1, source_target_pairs={{0,16},{8,24},{16,32},{24,40},{32,48},{40,56},{48,64},{56,72},{64,... | collective-permute-start | bytes 393224 | tf_op jit(solution)/shard_map/ppermute | solution.py:13
  20.2 4.5 %collective-permute-start.3 = (bf16[512,1,128]{0,2,1:T(8,128)(2,1)}, bf16[512,1,128]{0,2,1:T(8,128)(2,1)}, u32[]{:S(2)}, u32[]{:S(2)}) collective-permute-start(bf16[512,1,128]{0,2,1:T(8,128)(2,1)} %pad_maximum_fusion), channel_id=1, source_target_pairs={{0,8},{8,16},{16,24},{24,32},{32,40},{40,48},{48,56},{56,64},{64,7... | collective-permute-start | bytes 393224 | tf_op jit(solution)/shard_map/ppermute | solution.py:13
  24.7 2.2 %convolution_convert_fusion.1 = bf16[512,128]{1,0:T(8,128)(2,1)} fusion(bf16[512,5376]{1,0:T(8,128)(2,1)S(1)} %copy-done.1, bf16[5376,128]{1,0:T(8,128)(2,1)S(1)} %copy-done.8), kind=kOutput, calls=%fused_computation.15 | convolution fusion | flops 704708608 | bytes 7012352 | tf_op jit(solution)/shard_map/dot_general | solution.py:89
  27.0 4.9 %collective-permute-start = (bf16[512,128]{1,0:T(8,128)(2,1)}, bf16[512,128]{1,0:T(8,128)(2,1)}, u32[]{:S(2)}, u32[]{:S(2)}) collective-permute-start(bf16[512,128]{1,0:T(8,128)(2,1)} %convolution_convert_fusion.1), channel_id=1, source_target_pairs={{0,16},{8,24},{16,32},{24,40},{32,48},{40,56},{48,64},{56,72},{64,... | collective-permute-start | bytes 393224 | tf_op jit(solution)/shard_map/ppermute | solution.py:13
  31.8 3.6 %collective-permute-start.1 = (bf16[512,128]{1,0:T(8,128)(2,1)}, bf16[512,128]{1,0:T(8,128)(2,1)}, u32[]{:S(2)}, u32[]{:S(2)}) collective-permute-start(bf16[512,128]{1,0:T(8,128)(2,1)} %convolution_convert_fusion.1), channel_id=1, source_target_pairs={{0,8},{8,16},{16,24},{24,32},{32,40},{40,48},{48,56},{56,64},{64,7... | collective-permute-start | bytes 393224 | tf_op jit(solution)/shard_map/ppermute | solution.py:13
  35.5 1.2 reduce-window.20
  37.3 3.5 %fusion.6 = bf16[1024,672]{0,1:T(8,128)(2,1)} fusion(s32[512]{0:T(512)S(1)} %multiply_add_fusion, bf16[512,5376]{1,0:T(8,128)(2,1)} %param.10, s32[]{:T(128)S(6)} %select_n.12), kind=kOutput, calls=%fused_computation.11 | convolution fusion | flops 705855488 | bytes 2164740 | tf_op jit(solution)/shard_map/dot_general | solution.py:74
  40.9 2.5 %copy.35 = bf16[1024,672]{1,0:T(8,128)(2,1)} copy(bf16[1024,672]{0,1:T(8,128)(2,1)} %fusion.6) | data formatting | bytes 2752512 | tf_op jit(solution)/shard_map/convert_element_type | solution.py:74
  43.5 1.8 multiply_cosine_fusion
  46.0 5.0 %fusion.47 = f32[512,256]{0,1:T(8,128)} fusion(bf16[512,5376]{1,0:T(8,128)(2,1)} %param.10, bf16[5376,256]{1,0:T(8,128)(2,1)S(1)} %copy-done), kind=kOutput, calls=%fused_computation.78 | convolution fusion | flops 1409286144 | bytes 8781824 | tf_op jit(solution)/shard_map/dot_general | solution.py:87
  51.0 41.4 %all-gather.3.cloned.1.call-done = bf16[32,672,64]{1,2,0:T(8,128)(2,1)} async-done(((bf16[1,672,64]{1,2,0:T(8,128)(2,1)}), bf16[32,672,64]{1,2,0:T(8,128)(2,1)}) %all-gather.3.cloned.1.call-update) | async-done | bytes 2752528 | tf_op jit(solution)/shard_map/all_gather | solution.py:76
  92.4 4.1 %fusion.48 = f32[32,32,64]{2,1,0:T(8,128)} fusion(bf16[32,32,672]{2,1,0:T(8,128)(2,1)} %bitcast.74, bf16[32,672,64]{1,2,0:T(8,128)(2,1)} %all-gather.3.cloned.1.call-done), kind=kOutput, calls=%fused_computation.79 | convolution fusion | flops 88080384 | bytes 4390912 | tf_op jit(solution)/shard_map/acd,adr->acr/dot_general | solution.py:80
  96.5 27.3 %all-reduce.1 = bf16[32,32,64]{2,1,0:T(8,128)(2,1)} all-reduce(f32[32,32,64]{2,1,0:T(8,128)} %fusion.48), channel_id=1, replica_groups=mesh['seq'=32,'tp'=8] {'tp'}, use_global_device_ids=true, to_apply=%region_6.7 | all-reduce | flops 65536 | bytes 393216 | tf_op jit(solution)/shard_map/psum | solution.py:81
  123.8 44.2 %all-gather.5.cloned.1.call-done = bf16[32,64,256]{2,1,0:T(8,128)(2,1)} async-done(((bf16[1,64,256]{2,1,0:T(8,128)(2,1)}), bf16[32,64,256]{2,1,0:T(8,128)(2,1)}) %all-gather.5.cloned.1.call-update) | async-done | bytes 1048592 | tf_op jit(solution)/shard_map/all_gather | solution.py:77
  167.9 1.6 convolution_convert_fusion
  169.6 2.5 %multiply_reduce_fusion = (f32[512,2]{0,1:T(2,128)S(1)}, f32[512,256]{0,1:T(8,128)}) fusion(f32[512,256]{0,1:T(8,128)} %fusion.47, bf16[1024,256]{1,0:T(8,128)(2,1)S(1)} %bitcast.75, s32[512]{0:T(512)S(1)} %multiply_add_fusion), kind=kOutput, calls=%fused_computation.22 | convolution fusion | flops 269351936 | bytes 1579008 | tf_op jit(solution)/shard_map/st,se->te/dot_general | solution.py:86
  172.0 2.0 %copy.36 = f32[512,2,128]{2,0,1:T(8,128)} copy(f32[512,2,128]{0,2,1:T(8,128)} %bitcast.76) | data formatting | bytes 1048576 | tf_op jit(solution)/shard_map/reshape | solution.py:93
  174.1 1.2 divide_multiply_fusion
  175.3 1.3 subtract_convert_fusion
  176.6 2.7 %fusion.1 = (f32[2,512]{1,0:T(2,128)S(1)}, f32[1536,512,2]{1,0,2:T(8,128)S(1)}) fusion(pred[512,1536]{0,1:T(8,128)(4,1)S(1)} %compare_and_fusion, bf16[512,2,64]{2,0,1:T(8,128)(2,1)S(1)} %get-tuple-element.6, bf16[512,2,64]{2,0,1:T(8,128)(2,1)S(1)} %get-tuple-element.5, bf16[512,1,64]{0,2,1:T(8,128)(2,1)} %copy-done.3, bf16[512,1,64]{0,2,1:T(8,128)(2,1)} %copy-done.2, ...), kind=kOutput, calls=%fused_computation.4 | convolution fusion | flops 409467904 | bytes 7737344 | tf_op jit(solution)/shard_map/tkgd,skd->kgts/dot_general | solution.py:114
  179.3 1.5 fusion
  180.8 3.9 %fusion.8 = bf16[128,2,512]{2,0,1:T(8,128)(2,1)} fusion(f32[2,512]{1,0:T(2,128)S(1)} %fusion, f32[2,512]{1,0:T(2,128)S(1)} %get-tuple-element.15, f32[1536,512,2]{1,0,2:T(8,128)S(1)} %get-tuple-element.16, pred[512,1536]{0,1:T(8,128)(4,1)S(1)} %compare_and_fusion, bf16[512,128]{1,0:T(8,128)(2,1)} %convolution_convert_fusion.1, ...), kind=kOutput, calls=%fused_computation.14 | convolution fusion | flops 411828224 | bytes 7741440 | tf_op jit(solution)/shard_map/kgts,skd->tkgd/dot_general | solution.py:121
  184.7 1.8 copy.40
  (48 shorter events, 4.2 us)
Async XLA Ops:
  6.5 39.4 %copy-start = (bf16[5376,256]{1,0:T(8,128)(2,1)S(1)}, bf16[5376,256]{1,0:T(8,128)(2,1)}, u32[]{:S(2)}) copy-start(bf16[5376,256]{1,0:T(8,128)(2,1)} %param.11) | copy-start | bytes 8257540
  6.5 5.9 %copy-start.5 = (f32[128]{0:T(128)S(1)}, f32[128]{0:T(128)}, u32[]{:S(2)}) copy-start(f32[128]{0:T(128)} %param.15) | copy-start | bytes 1540
  6.5 85.9 %all-gather.3.cloned.1.call-start = ((), (), s32[]{:S(2)}) async-start(), calls=%async_computation | async-start | bytes 3244032 | tf_op jit(solution)/shard_map/all_gather | solution.py:76
  7.3 160.7 %all-gather.5.cloned.1.call-start = ((), (), s32[]{:S(2)}) async-start(), calls=%async_computation.1 | async-start | bytes 1081344 | tf_op jit(solution)/shard_map/all_gather | solution.py:77
  7.3 17.4 %copy-start.1 = (bf16[512,5376]{1,0:T(8,128)(2,1)S(1)}, bf16[512,5376]{1,0:T(8,128)(2,1)}, u32[]{:S(2)}) copy-start(bf16[512,5376]{1,0:T(8,128)(2,1)} %param.10) | copy-start | bytes 16515076
  7.4 17.4 %copy-start.8 = (bf16[5376,128]{1,0:T(8,128)(2,1)S(1)}, bf16[5376,128]{1,0:T(8,128)(2,1)}, u32[]{:S(2)}) copy-start(bf16[5376,128]{1,0:T(8,128)(2,1)} %param.13) | copy-start | bytes 4128772
  12.4 23.0 %copy-start.4 = (s32[512,1]{0,1:T(1,128)S(1)}, s32[512,1]{0,1:T(1,128)}, u32[]{:S(2)}) copy-start(s32[512,1]{0,1:T(1,128)} %param.18) | copy-start | bytes 6148
  12.4 24.6 %copy-start.7 = (s32[16]{0:T(128)S(1)}, s32[16]{0:T(128)}, u32[]{:S(2)}) copy-start(s32[16]{0:T(128)} %param.19) | copy-start | bytes 196
  13.1 0.6 copy-start.2
  13.2 1.3 copy-start.3
  14.4 162.2 %collective-permute-start.2 = (bf16[512,1,128]{0,2,1:T(8,128)(2,1)}, bf16[512,1,128]{0,2,1:T(8,128)(2,1)}, u32[]{:S(2)}, u32[]{:S(2)}) collective-permute-start(bf16[512,1,128]{0,2,1:T(8,128)(2,1)} %pad_maximum_fusion), channel_id=1, source_target_pairs={{0,16},{8,24},{16,32},{24,40},{32,48},{40,56},{48,64},{56,72},{64,... | collective-permute-start | bytes 393224 | tf_op jit(solution)/shard_map/ppermute | solution.py:13
  20.2 156.4 %collective-permute-start.3 = (bf16[512,1,128]{0,2,1:T(8,128)(2,1)}, bf16[512,1,128]{0,2,1:T(8,128)(2,1)}, u32[]{:S(2)}, u32[]{:S(2)}) collective-permute-start(bf16[512,1,128]{0,2,1:T(8,128)(2,1)} %pad_maximum_fusion), channel_id=1, source_target_pairs={{0,8},{8,16},{16,24},{24,32},{32,40},{40,48},{48,56},{56,64},{64,7... | collective-permute-start | bytes 393224 | tf_op jit(solution)/shard_map/ppermute | solution.py:13
  27.0 153.8 %collective-permute-start = (bf16[512,128]{1,0:T(8,128)(2,1)}, bf16[512,128]{1,0:T(8,128)(2,1)}, u32[]{:S(2)}, u32[]{:S(2)}) collective-permute-start(bf16[512,128]{1,0:T(8,128)(2,1)} %convolution_convert_fusion.1), channel_id=1, source_target_pairs={{0,16},{8,24},{16,32},{24,40},{32,48},{40,56},{48,64},{56,72},{64,... | collective-permute-start | bytes 393224 | tf_op jit(solution)/shard_map/ppermute | solution.py:13
  31.8 149.0 %collective-permute-start.1 = (bf16[512,128]{1,0:T(8,128)(2,1)}, bf16[512,128]{1,0:T(8,128)(2,1)}, u32[]{:S(2)}, u32[]{:S(2)}) collective-permute-start(bf16[512,128]{1,0:T(8,128)(2,1)} %convolution_convert_fusion.1), channel_id=1, source_target_pairs={{0,8},{8,16},{16,24},{24,32},{32,40},{40,48},{48,56},{56,64},{64,7... | collective-permute-start | bytes 393224 | tf_op jit(solution)/shard_map/ppermute | solution.py:13
  51.0 123.1 %copy-start.6 = (f32[128]{0:T(128)S(1)}, f32[128]{0:T(128)}, u32[]{:S(2)}) copy-start(f32[128]{0:T(128)} %param.14) | copy-start | bytes 1540
Sparse Core Ops, SparseCore 0:
  9.9 82.4 all-gather.2
  95.0 72.9 all-gather.4
where the time goes:
time: 194 us; the launch traced here: 193 us
  waiting for transfers between devices  86.3 us (44%)
  matrix products  30.6 us (16%)
  blocking collectives  27.3 us (14%)
  starting transfers between devices  18.8 us (10%)
  between operations  13.6 us (7%)
  other arithmetic  9.43 us (5%)
  local copies, waits for them, and re-layouts  7.32 us (4%)
    all_gather x1, waiting for transfers between devices, body(): lax.all_gather(adapter_up_weight, 'seq', axis=0, tiled=True)  44.2 us
    all_gather x1, waiting for transfers between devices, body(): lax.all_gather(adapter_down_weight, 'seq', axis=0, tiled=True)  41.4 us
    psum x1, blocking collectives, body(): low_rank = lax.psum(partial_low, 'tp').astype(jnp.bfloat16)  27.3 us
    ppermute x4, starting transfers between devices, passed_along(): return lax.ppermute(block, axis, route)  18.7 us
    dot_general x1, matrix products, body(): keys = jnp.dot(tokens, key_weight, preferred_element_type=jnp.float32)  5.07 us
    dot_general x1, matrix products, body(): jnp.dot(tokens, query_weight, preferred_element_type=jnp.float32)  5.02 us
    dot_general x1, matrix products, body(): jnp.einsum('acd,adr->acr', packed, down_all, preferred_element_type=jnp.f...  4.11 us
    dot_general x1, matrix products, body(): jnp.einsum('kgts,skd->tkgd', probs, all_values, preferred_element_type=jn...  3.91 us
  transfers between devices with their start and end apart: 6, of which 2 were waited for; matrix products, arithmetic and copies ran while one was open for 21% of the time, Pallas kernels for 0%

commit v1 on v0

--- a/solution.py
+++ b/solution.py
@@ -74,7 +74,15 @@
     packed = jnp.dot(dispatch, x_part, preferred_element_type=jnp.float32).astype(jnp.bfloat16)
     down_all, up_all = (
         lax.all_gather(adapter_down_weight, "seq", axis=0, tiled=True),
-        lax.all_gather(adapter_up_weight, "seq", axis=0, tiled=True),
+        jnp.concatenate(
+            lax.all_to_all(
+                jnp.stack(lax.axis_size("seq") * [adapter_up_weight]),
+                split_axis=0,
+                concat_axis=0,
+                axis_name="seq",
+            ),
+            0,
+        ),
     )
     packed = packed.reshape(adapter_total, capacity, feature_slice)
     partial_low = jnp.einsum("acd,adr->acr", packed, down_all, preferred_element_type=jnp.float32)

time: 194 us -> 154 us (0.79)
  the two profiles are of different devices: /device:TPU:8 before, /device:TPU:6 now
where the time goes in v1:
time: 154 us; the launch traced here: 153 us
  waiting for transfers between devices  34.6 us (22%)
  blocking collectives  31.2 us (20%)
  matrix products  30.6 us (20%)
  starting transfers between devices  25.2 us (16%)
  between operations  13.7 us (9%)
  other arithmetic  9.46 us (6%)
  local copies, waits for them, and re-layouts  8.42 us (5%)
    all_gather x1, waiting for transfers between devices, body(): lax.all_gather(adapter_down_weight, 'seq', axis=0, tiled=True)  33.8 us
    psum x1, blocking collectives, body(): low_rank = lax.psum(partial_low, 'tp').astype(jnp.bfloat16)  31.2 us
    ppermute x4, starting transfers between devices, passed_along(): return lax.ppermute(block, axis, route)  17.4 us
    all_to_all x1, starting transfers between devices, body(): lax.all_to_all(jnp.stack(lax.axis_size('seq') * [adapter_up_weight]), spl...  7.77 us
    dot_general x1, matrix products, body(): keys = jnp.dot(tokens, key_weight, preferred_element_type=jnp.float32)  5.07 us
    dot_general x1, matrix products, body(): jnp.dot(tokens, query_weight, preferred_element_type=jnp.float32)  5.01 us
    dot_general x1, matrix products, body(): jnp.einsum('acd,adr->acr', packed, down_all, preferred_element_type=jnp.f...  4.11 us
    dot_general x1, matrix products, body(): jnp.einsum('kgts,skd->tkgd', probs, all_values, preferred_element_type=jn...  3.91 us
  transfers between devices with their start and end apart: 6, of which 1 were waited for; matrix products, arithmetic and copies ran while one was open for 28% of the time, Pallas kernels for 0%

profile of v1, /device:TPU:6, one launch (start us, length us, event | category | flops | bytes accessed | tf_op | source)
XLA Modules:
  0.0 153.2 jit_solution(9365310058817768473)
XLA Ops:
  7.3 5.1 %multiply_reduce_fusion.1 = (f32[512]{0:T(512)S(1)}, f32[512,128]{0,1:T(8,128)S(1)}) fusion(bf16[512,5376]{1,0:T(8,128)(2,1)} %param.10, bf16[5376,128]{1,0:T(8,128)(2,1)} %param.12), kind=kOutput, calls=%fused_computation.44 | convolution fusion | flops 704773632 | bytes 7145472 | tf_op jit(solution)/shard_map/dot_general | solution.py:96
  14.4 5.2 %collective-permute-start.2 = (bf16[512,1,128]{0,2,1:T(8,128)(2,1)}, bf16[512,1,128]{0,2,1:T(8,128)(2,1)}, u32[]{:S(2)}, u32[]{:S(2)}) collective-permute-start(bf16[512,1,128]{0,2,1:T(8,128)(2,1)} %pad_maximum_fusion), channel_id=1, source_target_pairs={{0,16},{8,24},{16,32},{24,40},{32,48},{40,56},{48,64},{56,72},{64,... | collective-permute-start | bytes 393224 | tf_op jit(solution)/shard_map/ppermute | solution.py:13
  19.6 3.8 %collective-permute-start.3 = (bf16[512,1,128]{0,2,1:T(8,128)(2,1)}, bf16[512,1,128]{0,2,1:T(8,128)(2,1)}, u32[]{:S(2)}, u32[]{:S(2)}) collective-permute-start(bf16[512,1,128]{0,2,1:T(8,128)(2,1)} %pad_maximum_fusion), channel_id=1, source_target_pairs={{0,8},{8,16},{16,24},{24,32},{32,40},{40,48},{48,56},{56,64},{64,7... | collective-permute-start | bytes 393224 | tf_op jit(solution)/shard_map/ppermute | solution.py:13
  23.4 2.2 %convolution_convert_fusion.1 = bf16[512,128]{1,0:T(8,128)(2,1)} fusion(bf16[512,5376]{1,0:T(8,128)(2,1)S(1)} %copy-done.1, bf16[5376,128]{1,0:T(8,128)(2,1)S(1)} %copy-done.9), kind=kOutput, calls=%fused_computation.15 | convolution fusion | flops 704708608 | bytes 7012352 | tf_op jit(solution)/shard_map/dot_general | solution.py:97
  25.7 5.5 %collective-permute-start = (bf16[512,128]{1,0:T(8,128)(2,1)}, bf16[512,128]{1,0:T(8,128)(2,1)}, u32[]{:S(2)}, u32[]{:S(2)}) collective-permute-start(bf16[512,128]{1,0:T(8,128)(2,1)} %convolution_convert_fusion.1), channel_id=1, source_target_pairs={{0,16},{8,24},{16,32},{24,40},{32,48},{40,56},{48,64},{56,72},{64,... | collective-permute-start | bytes 393224 | tf_op jit(solution)/shard_map/ppermute | solution.py:13
  31.1 2.9 %collective-permute-start.1 = (bf16[512,128]{1,0:T(8,128)(2,1)}, bf16[512,128]{1,0:T(8,128)(2,1)}, u32[]{:S(2)}, u32[]{:S(2)}) collective-permute-start(bf16[512,128]{1,0:T(8,128)(2,1)} %convolution_convert_fusion.1), channel_id=1, source_target_pairs={{0,8},{8,16},{16,24},{24,32},{32,40},{40,48},{48,56},{56,64},{64,7... | collective-permute-start | bytes 393224 | tf_op jit(solution)/shard_map/ppermute | solution.py:13
  35.2 7.8 %all-to-all-start = ((bf16[32,1,64,256]{3,2,1,0:T(8,128)(2,1)}), bf16[32,1,64,256]{3,2,1,0:T(8,128)(2,1)}, u32[]{:S(2)}, u32[]{:S(2)}) async-start(bf16[32,1,64,256]{3,2,1,0:T(8,128)(2,1)} %stack.2), calls=%async_computation | async-start | bytes 2097152 | tf_op jit(solution)/shard_map/all_to_all | solution.py:78
  43.0 1.2 reduce-window.20
  44.9 3.6 %fusion.6 = bf16[1024,672]{0,1:T(8,128)(2,1)} fusion(s32[512]{0:T(512)S(1)} %multiply_add_fusion, bf16[512,5376]{1,0:T(8,128)(2,1)} %param.10, s32[]{:T(128)S(6)} %select_n.12), kind=kOutput, calls=%fused_computation.11 | convolution fusion | flops 705855488 | bytes 2164740 | tf_op jit(solution)/shard_map/dot_general | solution.py:74
  48.4 2.5 %copy.35 = bf16[1024,672]{1,0:T(8,128)(2,1)} copy(bf16[1024,672]{0,1:T(8,128)(2,1)} %fusion.6) | data formatting | bytes 2752512 | tf_op jit(solution)/shard_map/convert_element_type | solution.py:74
  51.0 1.8 %multiply_cosine_fusion = (f32[512,64]{1,0:T(8,128)}, f32[512,64]{1,0:T(8,128)}) fusion(f32[64]{0:T(128)S(1)} %multiply_exponential_fusion, f32[512]{0:T(512)S(1)} %fusion.42), kind=kLoop, calls=%fused_computation.38 | loop fusion | flops 32768 | bytes 264448 | tf_op jit(solution)/shard_map/cos | solution.py:39
  53.5 5.0 %fusion.48 = f32[512,256]{0,1:T(8,128)} fusion(bf16[512,5376]{1,0:T(8,128)(2,1)} %param.10, bf16[5376,256]{1,0:T(8,128)(2,1)S(1)} %copy-done), kind=kOutput, calls=%fused_computation.79 | convolution fusion | flops 1409286144 | bytes 8781824 | tf_op jit(solution)/shard_map/dot_general | solution.py:95
  58.5 33.8 %all-gather.2.cloned.1.call-done = bf16[32,672,64]{1,2,0:T(8,128)(2,1)} async-done(((bf16[1,672,64]{1,2,0:T(8,128)(2,1)}), bf16[32,672,64]{1,2,0:T(8,128)(2,1)}) %all-gather.2.cloned.1.call-update) | async-done | bytes 2752528 | tf_op jit(solution)/shard_map/all_gather | solution.py:76
  92.4 4.1 %fusion.49 = f32[32,32,64]{2,1,0:T(8,128)} fusion(bf16[32,32,672]{2,1,0:T(8,128)(2,1)} %bitcast.77, bf16[32,672,64]{1,2,0:T(8,128)(2,1)} %all-gather.2.cloned.1.call-done), kind=kOutput, calls=%fused_computation.80 | convolution fusion | flops 88080384 | bytes 4390912 | tf_op jit(solution)/shard_map/acd,adr->acr/dot_general | solution.py:88
  96.5 31.2 %all-reduce.1 = bf16[32,32,64]{2,1,0:T(8,128)(2,1)} all-reduce(f32[32,32,64]{2,1,0:T(8,128)} %fusion.49), channel_id=1, replica_groups=mesh['seq'=32,'tp'=8] {'tp'}, use_global_device_ids=true, to_apply=%region_6.7 | all-reduce | flops 65536 | bytes 393216 | tf_op jit(solution)/shard_map/psum | solution.py:89
  127.7 1.6 %convolution_convert_fusion = bf16[32,32,256]{2,1,0:T(8,128)(2,1)S(1)} fusion(bf16[32,1,64,256]{3,2,1,0:T(8,128)(2,1)} %all-to-all-done, bf16[32,32,64]{2,1,0:T(8,128)(2,1)} %all-reduce.1), kind=kOutput, calls=%fused_computation.12 | convolution fusion | flops 33816576 | bytes 1703936 | tf_op jit(solution)/shard_map/acr,are->ace/dot_general | solution.py:90
  129.4 2.5 %multiply_reduce_fusion = (f32[512,2]{0,1:T(2,128)S(1)}, f32[512,256]{0,1:T(8,128)}) fusion(f32[512,256]{0,1:T(8,128)} %fusion.48, bf16[1024,256]{1,0:T(8,128)(2,1)S(1)} %bitcast.78, s32[512]{0:T(512)S(1)} %multiply_add_fusion), kind=kOutput, calls=%fused_computation.23 | convolution fusion | flops 269351936 | bytes 1579008 | tf_op jit(solution)/shard_map/st,se->te/dot_general | solution.py:94
  131.8 2.0 %copy.36 = f32[512,2,128]{2,0,1:T(8,128)} copy(f32[512,2,128]{0,2,1:T(8,128)} %bitcast.79) | data formatting | bytes 1048576 | tf_op jit(solution)/shard_map/reshape | solution.py:101
  133.9 1.2 divide_multiply_fusion
  135.1 1.3 subtract_convert_fusion
  136.4 2.7 %fusion.1 = (f32[2,512]{1,0:T(2,128)S(1)}, f32[1536,512,2]{1,0,2:T(8,128)S(1)}) fusion(pred[512,1536]{0,1:T(8,128)(4,1)S(1)} %compare_and_fusion, bf16[512,2,64]{2,0,1:T(8,128)(2,1)S(1)} %get-tuple-element.6, bf16[512,2,64]{2,0,1:T(8,128)(2,1)S(1)} %get-tuple-element.5, bf16[512,1,64]{0,2,1:T(8,128)(2,1)} %copy-done.3, bf16[512,1,64]{0,2,1:T(8,128)(2,1)} %copy-done.2, ...), kind=kOutput, calls=%fused_computation.4 | convolution fusion | flops 409467904 | bytes 7737344 | tf_op jit(solution)/shard_map/tkgd,skd->kgts/dot_general | solution.py:122
  139.1 1.5 fusion
  140.6 3.9 %fusion.8 = bf16[128,2,512]{2,0,1:T(8,128)(2,1)} fusion(f32[2,512]{1,0:T(2,128)S(1)} %fusion, f32[2,512]{1,0:T(2,128)S(1)} %get-tuple-element.15, f32[1536,512,2]{1,0,2:T(8,128)S(1)} %get-tuple-element.16, pred[512,1536]{0,1:T(8,128)(4,1)S(1)} %compare_and_fusion, bf16[512,128]{1,0:T(8,128)(2,1)} %convolution_convert_fusion.1, ...), kind=kOutput, calls=%fused_computation.14 | convolution fusion | flops 411828224 | bytes 7741440 | tf_op jit(solution)/shard_map/kgts,skd->tkgd/dot_general | solution.py:129
  144.5 1.8 %copy.40 = bf16[512,256]{1,0:T(8,128)(2,1)} copy(bf16[512,256]{0,1:T(8,128)(2,1)} %bitcast.80) | data formatting | bytes 524288 | tf_op jit(solution)/shard_map/reshape | solution.py:130
  (50 shorter events, 5.2 us)
Async XLA Ops:
  6.5 47.0 %copy-start = (bf16[5376,256]{1,0:T(8,128)(2,1)S(1)}, bf16[5376,256]{1,0:T(8,128)(2,1)}, u32[]{:S(2)}) copy-start(bf16[5376,256]{1,0:T(8,128)(2,1)} %param.11) | copy-start | bytes 8257540
  6.5 5.9 %copy-start.6 = (f32[128]{0:T(128)S(1)}, f32[128]{0:T(128)}, u32[]{:S(2)}) copy-start(f32[128]{0:T(128)} %param.15) | copy-start | bytes 1540
  6.5 85.9 %all-gather.2.cloned.1.call-start = ((), (), s32[]{:S(2)}) async-start(), calls=%async_computation.1 | async-start | bytes 3244032 | tf_op jit(solution)/shard_map/all_gather | solution.py:76
  7.3 16.1 %copy-start.1 = (bf16[512,5376]{1,0:T(8,128)(2,1)S(1)}, bf16[512,5376]{1,0:T(8,128)(2,1)}, u32[]{:S(2)}) copy-start(bf16[512,5376]{1,0:T(8,128)(2,1)} %param.10) | copy-start | bytes 16515076
  7.3 16.1 %copy-start.9 = (bf16[5376,128]{1,0:T(8,128)(2,1)S(1)}, bf16[5376,128]{1,0:T(8,128)(2,1)}, u32[]{:S(2)}) copy-start(bf16[5376,128]{1,0:T(8,128)(2,1)} %param.13) | copy-start | bytes 4128772
  12.4 21.7 %copy-start.4 = (bf16[1,64,256]{2,1,0:T(8,128)(2,1)S(1)}, bf16[1,64,256]{2,1,0:T(8,128)(2,1)}, u32[]{:S(2)}) copy-start(bf16[1,64,256]{2,1,0:T(8,128)(2,1)} %param.17) | copy-start | bytes 98308
  12.5 30.4 %copy-start.5 = (s32[512,1]{0,1:T(1,128)S(1)}, s32[512,1]{0,1:T(1,128)}, u32[]{:S(2)}) copy-start(s32[512,1]{0,1:T(1,128)} %param.18) | copy-start | bytes 6148
  13.1 0.6 copy-start.2
  13.1 1.3 copy-start.3
  13.1 31.3 %copy-start.8 = (s32[16]{0:T(128)S(1)}, s32[16]{0:T(128)}, u32[]{:S(2)}) copy-start(s32[16]{0:T(128)} %param.19) | copy-start | bytes 196
  14.4 122.0 %collective-permute-start.2 = (bf16[512,1,128]{0,2,1:T(8,128)(2,1)}, bf16[512,1,128]{0,2,1:T(8,128)(2,1)}, u32[]{:S(2)}, u32[]{:S(2)}) collective-permute-start(bf16[512,1,128]{0,2,1:T(8,128)(2,1)} %pad_maximum_fusion), channel_id=1, source_target_pairs={{0,16},{8,24},{16,32},{24,40},{32,48},{40,56},{48,64},{56,72},{64,... | collective-permute-start | bytes 393224 | tf_op jit(solution)/shard_map/ppermute | solution.py:13
  19.6 116.8 %collective-permute-start.3 = (bf16[512,1,128]{0,2,1:T(8,128)(2,1)}, bf16[512,1,128]{0,2,1:T(8,128)(2,1)}, u32[]{:S(2)}, u32[]{:S(2)}) collective-permute-start(bf16[512,1,128]{0,2,1:T(8,128)(2,1)} %pad_maximum_fusion), channel_id=1, source_target_pairs={{0,8},{8,16},{16,24},{24,32},{32,40},{40,48},{48,56},{56,64},{64,7... | collective-permute-start | bytes 393224 | tf_op jit(solution)/shard_map/ppermute | solution.py:13
  25.7 114.9 %collective-permute-start = (bf16[512,128]{1,0:T(8,128)(2,1)}, bf16[512,128]{1,0:T(8,128)(2,1)}, u32[]{:S(2)}, u32[]{:S(2)}) collective-permute-start(bf16[512,128]{1,0:T(8,128)(2,1)} %convolution_convert_fusion.1), channel_id=1, source_target_pairs={{0,16},{8,24},{16,32},{24,40},{32,48},{40,56},{48,64},{56,72},{64,... | collective-permute-start | bytes 393224 | tf_op jit(solution)/shard_map/ppermute | solution.py:13
  31.1 109.5 %collective-permute-start.1 = (bf16[512,128]{1,0:T(8,128)(2,1)}, bf16[512,128]{1,0:T(8,128)(2,1)}, u32[]{:S(2)}, u32[]{:S(2)}) collective-permute-start(bf16[512,128]{1,0:T(8,128)(2,1)} %convolution_convert_fusion.1), channel_id=1, source_target_pairs={{0,8},{8,16},{16,24},{24,32},{32,40},{40,48},{48,56},{56,64},{64,7... | collective-permute-start | bytes 393224 | tf_op jit(solution)/shard_map/ppermute | solution.py:13
  35.2 92.6 %all-to-all-start = ((bf16[32,1,64,256]{3,2,1,0:T(8,128)(2,1)}), bf16[32,1,64,256]{3,2,1,0:T(8,128)(2,1)}, u32[]{:S(2)}, u32[]{:S(2)}) async-start(bf16[32,1,64,256]{3,2,1,0:T(8,128)(2,1)} %stack.2), calls=%async_computation | async-start | bytes 2097152 | tf_op jit(solution)/shard_map/all_to_all | solution.py:78
  58.5 75.3 %copy-start.7 = (f32[128]{0:T(128)S(1)}, f32[128]{0:T(128)}, u32[]{:S(2)}) copy-start(f32[128]{0:T(128)} %param.14) | copy-start | bytes 1540
Sparse Core Ops, SparseCore 0:
  9.9 82.4 all-gather.1
